TPU v7x, 256 devices: a whole 4x4x8 slice. The times are simulated.
256 devices in a mesh: section: 4 (over z_hi, core), kv: 16 (over z_lo, y), tp: 4 (over x).
Axes of the slice: x: 4, y: 4, z: 8 (z_hi: 2, z_lo: 4; z = z_hi * 4 + z_lo), core: 2. Of those that a mesh axis runs over, the one named last changes fastest.
Arguments:
- patches: bfloat16 [32768, 1152], P(('section', 'kv'), 'tp'), may hold values from -6 to 6
- vis_gain: float32 [1152], replicated, may hold values from 0.1 to 1.9
- vis_bias: float32 [1152], replicated, may hold values from -3 to 3
- w_proj: bfloat16 [1152, 4608], P('section', 'tp')
- b_proj: float32 [4608], P('tp'), may hold values from -12 to 12
- rms_gain: float32 [4608], P('tp'), may hold values from 0.1 to 1.9
- w_kv: bfloat16 [4608, 2, 1024], P('tp'), may hold values from -0.09375 to 0.09375
- queries: bfloat16 [16, 2048], P('section', 'tp'), may hold values from -18 to 18
- cache: bfloat16 [1024, 128, 2, 1024], P(('section', 'kv'), None, None, 'tp'), may hold values from -6 to 6
- cache_lengths: int32 [4, 4], P('section'), may hold values from 1 to 31872, 32256 in all within a row
- slot_page: int32 [4, 256], P('section', 'kv'), may hold values from 0 to 255, each once within a row
- page_owner: int32 [4, 64], replicated, may hold values from 0 to 15, as said below
- image_request: int32 [4, 2], P('section'), may hold values from 0 to 3
Outputs:
- new_pages: bfloat16 [2048, 128, 2, 1024], P(('section', 'kv'), None, None, 'tp')
- attended: bfloat16 [16, 2048], P('section', 'tp')
Inputs may be any that keep to these rules, and one draw needn't show every extreme that they name: `page_owner`: from each source's 4 pages at most 2 go to any one owner; in every group one owner receives exactly 2 pages from every source.
All inputs are finite; a program needn't handle non-finite values.
Results may differ from a plain program's by a relative error of at most 0.0063.
Values may be sent and summed in bfloat16 or wider, within the bound.
No kernel may reach another device: no remote copies, remote signals or barrier semaphores. Data moves between devices by JAX's collectives and lax.ppermute only.
A program may use at most 64 MiB of HBM per device.

v0:
```python
import jax
import jax.numpy as jnp
from jax import lax
from jax.sharding import PartitionSpec as P

HEAD_DIM = 128
IMAGE_PAGES = 32
query_scale = 1.0 / 12.0
softcap = 50.0
epsilon = 1e-06


def laid_out(parts, dim):
    parts = jnp.moveaxis(parts, 0, dim)
    lengths = parts.shape
    return parts.reshape(*lengths[:dim], lengths[dim] * lengths[dim + 1], *lengths[dim + 2 :])


def sent_to_all(x, axis):
    copies = jnp.broadcast_to(x, (lax.axis_size(axis), *x.shape))
    return lax.all_to_all(copies, axis, split_axis=0, concat_axis=0, tiled=True)


def gather_directly(x, axis, dim):
    return laid_out(sent_to_all(x, axis), dim)


def over_copies(x, axis):
    everything = sent_to_all(x, axis)
    return jnp.sum(everything, axis=0)


def cut_along(x, dim, devices):
    before, after = (x.shape[:dim], x.shape[dim + 1 :])
    return jnp.moveaxis(x.reshape(*before, devices, -1, *after), dim, 0)


def summed_on_arrival(x, axis, dim):
    devices = lax.axis_size(axis)
    parts = lax.all_to_all(cut_along(x, dim, devices), axis, 0, 0, tiled=True)
    return jnp.sum(parts, axis=0)


def from_behind(value, axis, steps):
    count = lax.axis_size(axis)
    pairs = [(source, (source + steps) % count) for source in range(count)]
    return lax.ppermute(value, axis, pairs)


def together(arrays, axis):
    ends = [0]
    for a in arrays:
        ends.append(ends[-1] + a.size)
    subtotal = over_copies(jnp.concatenate([a.ravel() for a in arrays]), axis)
    return tuple((subtotal[b:e].reshape(a.shape) for a, b, e in zip(arrays, ends, ends[1:])))


def block_ranks(owners):
    per_block = owners.shape[1]
    same_owner = owners[:, :, None] == owners[:, None, :]
    earlier = jnp.arange(per_block)[None, :] < jnp.arange(per_block)[:, None]
    return jnp.sum((same_owner & earlier[None, :, :]).astype(jnp.int32), axis=2)


def attend_part(query_grid, page_store, token_mask):
    slot_count = page_store.shape[0]
    page_len = page_store.shape[1]
    head_count = page_store.shape[3] // HEAD_DIM
    keys = page_store[:, :, 0, :].reshape(slot_count * page_len, head_count, HEAD_DIM)
    values = page_store[:, :, 1, :].reshape(slot_count * page_len, head_count, HEAD_DIM)
    raw_scores = jnp.einsum("rkgd,tkd->rkgt", query_grid, keys, preferred_element_type=jnp.float32)
    capped = softcap * jnp.tanh(raw_scores * query_scale / softcap)
    allowed = token_mask.reshape(slot_count * page_len, -1).T
    weights = jnp.where(allowed[:, None, None, :], jnp.exp(capped), jnp.float32(0.0))
    totals = jnp.sum(weights, axis=3)
    weighted = jnp.einsum(
        "rkgt,tkd->rkgd", weights.astype(jnp.bfloat16), values, preferred_element_type=jnp.float32
    )
    return (totals, weighted)


def per_device(
    patches,
    vis_gain,
    vis_bias,
    w_proj,
    b_proj,
    rms_gain,
    w_kv,
    queries,
    cache,
    cache_lengths,
    slot_page,
    page_owner,
    image_request,
):
    kv_count = lax.axis_size("kv")
    section_idx = lax.axis_index("section")
    kv_idx = lax.axis_index("kv")
    row_count = patches.shape[0]
    page_len = cache.shape[1]
    pages_dev = row_count // page_len
    capacity = max(2, (2 * pages_dev + kv_count - 1) // kv_count)
    recv_slots = kv_count * capacity
    gathered = gather_directly(patches, "tp", 1).astype(jnp.float32)
    row_mean = jnp.mean(gathered, axis=1, keepdims=True)
    centred = gathered - row_mean
    variance = jnp.mean(centred * centred, axis=1, keepdims=True)
    x_norm = (centred * lax.rsqrt(variance + epsilon) * vis_gain + vis_bias).astype(jnp.bfloat16)
    projected = (
        jnp.dot(
            x_norm,
            lax.all_gather(w_proj, "section", axis=0, tiled=True),
            preferred_element_type=jnp.float32,
        )
        + b_proj
    )
    squares = over_copies(jnp.sum(projected * projected, axis=1), "tp")
    full_width = projected.shape[1] * lax.axis_size("tp")
    hidden = (projected * lax.rsqrt(squares / full_width + epsilon)[:, None] * rms_gain).astype(
        jnp.bfloat16
    )
    partial_kv = jnp.einsum("nd,dcf->ncf", hidden, w_kv, preferred_element_type=jnp.float32)
    image_kv = summed_on_arrival(partial_kv, "tp", 2)
    kv_pages = image_kv.astype(jnp.bfloat16).reshape(pages_dev, page_len, 2, image_kv.shape[2])
    handed = from_behind(kv_pages, "section", 1)
    owners = lax.dynamic_index_in_dim(page_owner, section_idx, 0, keepdims=False).reshape(
        kv_count, pages_dev
    )
    page_ranks = block_ranks(owners)
    my_owner = lax.dynamic_index_in_dim(owners, kv_idx, 0, keepdims=False)
    my_rank = lax.dynamic_index_in_dim(page_ranks, kv_idx, 0, keepdims=False)
    target = my_owner * capacity + my_rank
    placing = (jnp.arange(recv_slots)[:, None] == target[None, :]).astype(jnp.bfloat16)
    new_pages = lax.all_to_all(
        jnp.einsum("jp,ptcf->jtcf", placing, handed, preferred_element_type=jnp.float32).astype(
            jnp.bfloat16
        ),
        "kv",
        split_axis=0,
        concat_axis=0,
        tiled=True,
    )
    req_count = queries.shape[0]
    kv_heads_dev = cache.shape[3] // HEAD_DIM
    group_size = queries.shape[1] // HEAD_DIM // kv_heads_dev
    query_grid = queries.reshape(req_count, kv_heads_dev, group_size, HEAD_DIM)
    lengths = cache_lengths[0]
    page_counts = (lengths + page_len - 1) // page_len
    starts = jnp.cumsum(page_counts) - page_counts
    slot_ids = slot_page[0]
    within = slot_ids[:, None] - starts[None, :]
    inside = (within >= 0) & (within < page_counts[None, :])
    valid = jnp.where(inside, jnp.clip(lengths[None, :] - within * page_len, 0, page_len), 0)
    cache_mask = jnp.arange(page_len)[None, :, None] < valid[:, None, :]
    cache_totals, cache_weighted = attend_part(query_grid, cache, cache_mask)
    own_owners = lax.dynamic_index_in_dim(page_owner, section_idx, 0, keepdims=False).reshape(
        kv_count, pages_dev
    )
    own_ranks = block_ranks(own_owners)
    slot_of = (jnp.arange(kv_count)[:, None] * capacity + own_ranks).reshape(-1)
    arrives_here = own_owners.reshape(-1) == kv_idx
    image_count = image_request.shape[1]
    image_of = jnp.arange(kv_count * pages_dev) // IMAGE_PAGES
    request_row = image_request[0]
    page_request = jnp.sum(
        jnp.where(image_of[:, None] == jnp.arange(image_count)[None, :], request_row[None, :], 0),
        axis=1,
    )
    matched = arrives_here[None, :] & (slot_of[None, :] == jnp.arange(recv_slots)[:, None])
    request_hit = page_request[:, None] == jnp.arange(req_count)[None, :]
    slot_request = jnp.any(matched[:, :, None] & request_hit[None, :, :], axis=1)
    image_mask = jnp.broadcast_to(slot_request[:, None, :], (recv_slots, page_len, req_count))
    image_totals, image_weighted = attend_part(query_grid, new_pages, image_mask)
    totals, weighted = together(
        (cache_totals + image_totals, cache_weighted + image_weighted), "kv"
    )
    attended = (weighted / totals[..., None]).astype(jnp.bfloat16).reshape(req_count, -1)
    return (new_pages, attended)


def solution(mesh):
    in_specs = (
        P(("section", "kv"), "tp"),
        P(),
        P(),
        P("section", "tp"),
        P("tp"),
        P("tp"),
        P("tp", None, None),
        P("section", "tp"),
        P(("section", "kv"), None, None, "tp"),
        P("section", None),
        P("section", "kv"),
        P(),
        P("section", None),
    )
    out_specs = (P(("section", "kv"), None, None, "tp"), P("section", "tp"))
    return jax.shard_map(
        per_device, mesh=mesh, in_specs=in_specs, out_specs=out_specs, check_vma=False
    )
```

profile of v0, /device:TPU:2, one launch (start us, length us, event | category | flops | bytes accessed | tf_op | source)
XLA Modules:
  0.0 313.6 jit_solution(7396003237262253135)
XLA Ops:
  7.2 0.0 copy-start
  7.2 0.0 all-gather.2.cloned.1.call-start
  7.2 0.7 all-gather.2.cloned.1.call-update
  7.9 1.0 broadcast_in_dim.44
  9.0 0.0 copy-start.3
  9.0 0.0 copy-start.4
  9.0 19.7 %all_to_all.27 = bf16[4,512,288]{1,2,0:T(8,128)(2,1)S(1)} all-to-all(bf16[4,512,288]{1,2,0:T(8,128)(2,1)S(1)} %broadcast_in_dim.44), channel_id=1, replica_groups=mesh['section'=4,'kv'=16,'tp'=4] {'tp'}, dimensions={0} | all-to-all | bytes 2359296 | tf_op jit(solution)/shard_map/all_to_all | solution.py:21
  28.7 0.2 convert_reduce_fusion
  28.9 0.4 multiply_reduce_fusion.1
  29.3 0.0 copy-done.3
  29.3 0.0 copy-done.4
  29.3 0.5 fusion.10
  29.8 32.4 %all-gather.2.cloned.1.call-done = bf16[1152,1152]{1,0:T(8,128)(2,1)} async-done(((bf16[288,1152]{1,0:T(8,128)(2,1)}), bf16[1152,1152]{1,0:T(8,128)(2,1)}) %all-gather.2.cloned.1.call-update) | async-done | bytes 2654224 | tf_op jit(solution)/shard_map/all_gather | solution.py:113
  62.2 0.0 copy-done.2
  62.2 3.8 %multiply_reduce_fusion = (f32[512]{0:T(512)S(1)}, f32[512,1152]{1,0:T(8,128)S(1)}) fusion(f32[1152]{0:T(1024)S(1)} %copy-done.2, bf16[512,1152]{0,1:T(8,128)(2,1)S(1)} %fusion.10, bf16[1152,1152]{1,0:T(8,128)(2,1)} %all-gather.2.cloned.1.call-done), kind=kOutput, calls=%fused_computation.19 | convolution fusion | flops 1360723456 | bytes 6199808 | tf_op jit(solution)/shard_map/dot_general | solution.py:111
  66.0 8.5 %all_to_all.28 = f32[4,1,512]{2,1,0:T(1,128)S(1)} all-to-all(f32[4,1,512]{2,1,0:T(1,128)S(1)} %broadcast_in_dim.45), channel_id=1, replica_groups=mesh['section'=4,'kv'=16,'tp'=4] {'tp'}, dimensions={0} | all-to-all | bytes 16384 | tf_op jit(solution)/shard_map/all_to_all | solution.py:21
  74.5 5.3 %fusion = f32[512,2,1024]{2,0,1:T(8,128)S(1)} fusion(bf16[1152,2,1024]{2,1,0:T(2,128)(2,1)} %param.19, f32[512,1152]{1,0:T(8,128)S(1)} %get-tuple-element.11, f32[1152]{0:T(1024)} %param.18, f32[512]{0:T(512)S(1)} %add_rsqrt_fusion), kind=kOutput, calls=%fused_computation | convolution fusion | flops 2417688576 | bytes 11278848 | tf_op jit(solution)/shard_map/nd,dcf->ncf/dot_general | solution.py:123
  79.8 0.4 copy.163
  80.2 51.5 %all_to_all.29 = f32[4,512,2,256]{3,1,2,0:T(8,128)} all-to-all(f32[4,512,2,256]{3,1,2,0:T(8,128)S(1)} %bitcast.89), channel_id=1, replica_groups=mesh['section'=4,'kv'=16,'tp'=4] {'tp'}, dimensions={0} | all-to-all | bytes 8388608 | tf_op jit(solution)/shard_map/all_to_all | solution.py:40
  131.7 2.5 reduce_sum.99
  134.2 0.4 copy.96
  134.6 0.3 collective-permute-start
  134.9 0.0 copy-done.7
  134.9 0.1 reshape.263
  135.0 0.1 copy.90
  135.1 0.1 convert_reduce_fusion.1
  135.2 0.2 add_reduce_fusion
  135.4 17.6 %collective-permute-done = bf16[4,128,2,256]{3,0,2,1:T(4,128)(2,1)S(1)} collective-permute-done((bf16[4,128,2,256]{3,0,2,1:T(4,128)(2,1)S(1)}, bf16[4,128,2,256]{3,0,2,1:T(4,128)(2,1)S(1)}, u32[]{:S(2)}, u32[]{:S(2)}) %collective-permute-start) | collective-permute-done | bytes 524320 | tf_op jit(solution)/shard_map/ppermute | solution.py:47
  153.0 1.4 convolution_convert_fusion
  154.3 6.3 %copy.97 = bf16[32,128,2,256]{3,2,1,0:T(2,128)(2,1)} copy(bf16[32,128,2,256]{3,0,2,1:T(8,128)(2,1)S(1)} %convolution_convert_fusion) | data formatting | bytes 8388608 | tf_op jit(solution)/shard_map/convert_element_type | solution.py:136
  160.7 4.9 %all-to-all-start.3 = ((bf16[32,128,2,256]{3,2,1,0:T(2,128)(2,1)}), bf16[32,128,2,256]{3,2,1,0:T(2,128)(2,1)}, u32[]{:S(2)}, u32[]{:S(2)}) async-start(bf16[32,128,2,256]{3,2,1,0:T(2,128)(2,1)} %copy.97), calls=%async_computation.3 | async-start | bytes 8388608 | tf_op jit(solution)/shard_map/all_to_all | solution.py:135
  165.6 0.1 copy.101
  165.7 0.1 add.113
  165.8 0.0 copy-done.8
  165.8 0.1 fusion.41
  165.9 0.2 and_reduce_fusion
  166.1 0.1 broadcast_bitcast_fusion
  166.2 0.0 copy-done.1
  166.2 0.0 copy-start.5
  166.2 10.0 %slice_reduce_fusion.3 = (bf16[16,128,256]{2,1,0:T(8,128)(2,1)}, bf16[16,128,256]{2,1,0:T(8,128)(2,1)S(1)}) fusion(bf16[16,128,2,256]{3,2,1,0:T(2,128)(2,1)S(1)} %copy-done.1), kind=kLoop, calls=%fused_computation.31 | loop fusion | bytes 4194304 | tf_op jit(solution)/shard_map/slice | solution.py:69
  176.2 1.4 reshape.276
  177.6 0.2 reduce-window_clone.1
  177.8 0.3 reshape.278
  178.1 0.1 fusion.37
  178.2 0.1 broadcast_bitcast_fusion.1
  178.3 0.5 fusion.44
  178.8 0.3 convolution_bitcast_fusion
  179.0 60.3 %all-to-all-done.3 = bf16[32,128,2,256]{3,2,1,0:T(2,128)(2,1)} async-done(((bf16[32,128,2,256]{3,2,1,0:T(2,128)(2,1)}), bf16[32,128,2,256]{3,2,1,0:T(2,128)(2,1)}, u32[]{:S(2)}, u32[]{:S(2)}) %all-to-all-start.3) | async-done | bytes 4194336 | tf_op jit(solution)/shard_map/all_to_all | solution.py:135
  239.3 21.9 %slice_reduce_fusion.1 = (bf16[32,128,256]{2,1,0:T(8,128)(2,1)S(1)}, bf16[32,128,256]{2,1,0:T(8,128)(2,1)}) fusion(bf16[32,128,2,256]{3,2,1,0:T(2,128)(2,1)} %all-to-all-done.3), kind=kLoop, calls=%fused_computation.10 | loop fusion | bytes 8388608 | tf_op jit(solution)/shard_map/slice | solution.py:69
  261.2 2.1 reshape.277
  263.3 2.5 reshape.279
  265.8 2.3 fusion.45
  268.2 0.4 fusion.26
  268.6 0.1 copy.105
  268.7 0.1 add.115
  268.8 0.1 pad_maximum_fusion
  268.9 0.1 broadcast_in_dim.54
  269.0 27.6 %all_to_all.30 = f32[16,1,2064]{2,1,0:T(1,128)S(1)} all-to-all(f32[16,1,2064]{2,1,0:T(1,128)S(1)} %broadcast_in_dim.54), channel_id=1, replica_groups=mesh['section'=4,'kv'=16,'tp'=4] {'kv'}, dimensions={0} | all-to-all | bytes 264192 | tf_op jit(solution)/shard_map/all_to_all | solution.py:21
  296.5 0.1 reduce_sum.103
  296.6 0.1 slice.34
  296.7 0.1 div.69
  296.8 0.1 div.70
  296.9 0.6 divide_convert_fusion
  297.5 9.2 %copy.166 = bf16[32,128,2,256]{3,2,1,0:T(2,128)(2,1)} copy(bf16[32,128,2,256]{3,2,1,0:T(2,128)(2,1)} %all-to-all-done.3) | data formatting | bytes 8388608
  (32 shorter events, 0.3 us)
Async XLA Ops:
  7.2 171.1 %copy-start = (bf16[4,512]{1,0:T(4,128)(2,1)S(1)}, bf16[4,512]{1,0:T(4,128)(2,1)}, u32[]{:S(2)}) copy-start(bf16[4,512]{1,0:T(4,128)(2,1)} %param.20) | copy-start | bytes 12292
  7.2 55.0 %all-gather.2.cloned.1.call-start = ((), (), s32[]{:S(2)}) async-start(), calls=%async_computation.5 | async-start | bytes 3317760 | tf_op jit(solution)/shard_map/all_gather | solution.py:113
  9.0 20.3 %copy-start.3 = (f32[1152]{0:T(1024)S(1)}, f32[1152]{0:T(1024)}, u32[]{:S(2)}) copy-start(f32[1152]{0:T(1024)} %param.15) | copy-start | bytes 13828
  9.0 20.3 %copy-start.4 = (f32[1152]{0:T(1024)S(1)}, f32[1152]{0:T(1024)}, u32[]{:S(2)}) copy-start(f32[1152]{0:T(1024)} %param.14) | copy-start | bytes 13828
  28.7 33.5 %copy-start.2 = (f32[1152]{0:T(1024)S(1)}, f32[1152]{0:T(1024)}, u32[]{:S(2)}) copy-start(f32[1152]{0:T(1024)} %param.17) | copy-start | bytes 13828
  131.6 3.2 %copy-start.7 = (s32[4,64]{1,0:T(4,128)S(1)}, s32[4,64]{1,0:T(4,128)}, u32[]{:S(2)}) copy-start(s32[4,64]{1,0:T(4,128)} %param.24) | copy-start | bytes 3076
  134.6 18.4 %collective-permute-start = (bf16[4,128,2,256]{3,0,2,1:T(4,128)(2,1)S(1)}, bf16[4,128,2,256]{3,0,2,1:T(4,128)(2,1)S(1)}, u32[]{:S(2)}, u32[]{:S(2)}) collective-permute-start(bf16[4,128,2,256]{3,0,2,1:T(4,128)(2,1)S(1)} %copy.96), channel_id=1, source_target_pairs={{0,64},{64,128},{128,192},{192,0},{1,65},{65,129},{129,193},{193,1... | collective-permute-start | bytes 1572872 | tf_op jit(solution)/shard_map/ppermute | solution.py:47
  160.7 5.1 %copy-start.8 = (s32[1,2]{1,0:T(1,128)S(1)}, s32[1,2]{1,0:T(1,128)}, u32[]{:S(2)}) copy-start(s32[1,2]{1,0:T(1,128)} %param.25) | copy-start | bytes 28
  160.7 5.5 %copy-start.1 = (bf16[16,128,2,256]{3,2,1,0:T(2,128)(2,1)S(1)}, bf16[16,128,2,256]{3,2,1,0:T(2,128)(2,1)}, u32[]{:S(2)}) copy-start(bf16[16,128,2,256]{3,2,1,0:T(2,128)(2,1)} %param.21) | copy-start | bytes 6291460
  160.7 78.6 %all-to-all-start.3 = ((bf16[32,128,2,256]{3,2,1,0:T(2,128)(2,1)}), bf16[32,128,2,256]{3,2,1,0:T(2,128)(2,1)}, u32[]{:S(2)}, u32[]{:S(2)}) async-start(bf16[32,128,2,256]{3,2,1,0:T(2,128)(2,1)} %copy.97), calls=%async_computation.3 | async-start | bytes 8388608 | tf_op jit(solution)/shard_map/all_to_all | solution.py:135
  166.2 11.3 %copy-start.5 = (s32[1,4]{1,0:T(1,128)S(1)}, s32[1,4]{1,0:T(1,128)}, u32[]{:S(2)}) copy-start(s32[1,4]{1,0:T(1,128)} %param.22) | copy-start | bytes 52
  176.2 1.9 copy-start.6
Sparse Core Ops, SparseCore 0:
  9.8 52.3 all-gather.1
where the time goes:
time: 314 us
  waiting for transfers between devices  111 us (35%)
  blocking collectives  107 us (34%)
  local copies, waits for them, and re-layouts  56.6 us (18%)
  between operations  14.4 us (5%)
  matrix products  14 us (4%)
  other arithmetic  5.3 us (2%)
  starting transfers between devices  5.19 us (2%)
    all_to_all x1, waiting for transfers between devices, per_device(): lax.all_to_all(jnp.einsum('jp,ptcf->jtcf', placing, handed, preferred_ele...  60.3 us
    all_to_all x3, blocking collectives, sent_to_all(): return lax.all_to_all(copies, axis, split_axis=0, concat_axis=0, tiled=True)  55.7 us
    all_to_all x1, blocking collectives, summed_on_arrival(): parts = lax.all_to_all(cut_along(x, dim, devices), axis, 0, 0, tiled=True)  51.5 us
    all_gather x1, waiting for transfers between devices, per_device(): lax.all_gather(w_proj, 'section', axis=0, tiled=True)  32.4 us
    slice x2, local copies, waits for them, and re-layouts, attend_part(): page_store[:, :, 0, :].reshape(slot_count * page_len, head_count, HEAD_DIM)  31.9 us
    ppermute x1, waiting for transfers between devices, from_behind(): return lax.ppermute(value, axis, pairs)  17.6 us
    unnamed x22, local copies, waits for them, and re-layouts  9.42 us
    convert_element_type x1, local copies, waits for them, and re-layouts, per_device(): jnp.einsum('jp,ptcf->jtcf', placing, handed, preferred_element_type=jnp.f...  6.33 us
  transfers between devices with their start and end apart: 3, of which 3 were waited for; matrix products, arithmetic and copies ran while one was open for 5% of the time, Pallas kernels for 0%

commit v1 on v0

--- a/solution.py
+++ b/solution.py
@@ -8,6 +8,11 @@
 query_scale = 1.0 / 12.0
 softcap = 50.0
 epsilon = 1e-06
+
+
+def exchange_gather(block, axis, dim):
+    sent = jnp.stack([block] * lax.axis_size(axis))
+    return jnp.concatenate(lax.all_to_all(sent, axis, 0, 0), axis=dim)
 
 
 def laid_out(parts, dim):
@@ -108,11 +113,7 @@
     variance = jnp.mean(centred * centred, axis=1, keepdims=True)
     x_norm = (centred * lax.rsqrt(variance + epsilon) * vis_gain + vis_bias).astype(jnp.bfloat16)
     projected = (
-        jnp.dot(
-            x_norm,
-            lax.all_gather(w_proj, "section", axis=0, tiled=True),
-            preferred_element_type=jnp.float32,
-        )
+        jnp.dot(x_norm, exchange_gather(w_proj, "section", 0), preferred_element_type=jnp.float32)
         + b_proj
     )
     squares = over_copies(jnp.sum(projected * projected, axis=1), "tp")

time: 314 us -> 338 us (1.076)
  starting transfers between devices: 5.19 us -> 32.9 us
  waiting for transfers between devices: 111 us -> 136 us
  blocking collectives: 107 us -> 87.8 us
  between operations: 14.4 us -> 0.96 us
    all_to_all x0 -> x1, waiting for transfers between devices: none -> 62.6 us  [exchange_gather(): return jnp.concatenate(lax.all_to_all(sent, axis, 0, 0), axis=dim)]
    all_gather x1 -> x0, waiting for transfers between devices: 32.4 us -> none  [per_device(): lax.all_gather(w_proj, 'section', axis=0, tiled=True)]
    all_to_all x1, starting transfers between devices: 4.89 us -> 24 us  [per_device(): lax.all_to_all(jnp.einsum('jp,ptcf->jtcf', placing, handed, preferred_ele...]
    all_to_all x1, blocking collectives: 51.5 us -> 33 us  [summed_on_arrival(): parts = lax.all_to_all(cut_along(x, dim, devices), axis, 0, 0, tiled=True)]
    all_to_all x0 -> x1, starting transfers between devices: none -> 8.59 us  [exchange_gather(): return jnp.concatenate(lax.all_to_all(sent, axis, 0, 0), axis=dim)]
    ppermute x1, waiting for transfers between devices: 17.6 us -> 12 us  [from_behind(): return lax.ppermute(value, axis, pairs)]
    unnamed x22 -> x26, local copies, waits for them, and re-layouts: 9.42 us -> 9.42 us
  transfers between devices with their start and end apart: 3 -> 3, of which waited for: 3 -> 3; matrix products, arithmetic and copies ran while one was open for 5% -> 4% of each run, Pallas kernels for 0% -> 0%
where the time goes in v1:
time: 338 us; the launch traced here: 337 us
  waiting for transfers between devices  136 us (40%)
  blocking collectives  87.8 us (26%)
  local copies, waits for them, and re-layouts  58.5 us (17%)
  starting transfers between devices  32.9 us (10%)
  matrix products  16.2 us (5%)
  other arithmetic  4.85 us (1%)
    all_to_all x1, waiting for transfers between devices, exchange_gather(): return jnp.concatenate(lax.all_to_all(sent, axis, 0, 0), axis=dim)  62.6 us
    all_to_all x1, waiting for transfers between devices, per_device(): lax.all_to_all(jnp.einsum('jp,ptcf->jtcf', placing, handed, preferred_ele...  61.4 us
    all_to_all x3, blocking collectives, sent_to_all(): return lax.all_to_all(copies, axis, split_axis=0, concat_axis=0, tiled=True)  54.7 us
    all_to_all x1, blocking collectives, summed_on_arrival(): parts = lax.all_to_all(cut_along(x, dim, devices), axis, 0, 0, tiled=True)  33 us
    slice x2, local copies, waits for them, and re-layouts, attend_part(): page_store[:, :, 0, :].reshape(slot_count * page_len, head_count, HEAD_DIM)  31.9 us
    all_to_all x1, starting transfers between devices, per_device(): lax.all_to_all(jnp.einsum('jp,ptcf->jtcf', placing, handed, preferred_ele...  24 us
    ppermute x1, waiting for transfers between devices, from_behind(): return lax.ppermute(value, axis, pairs)  12 us
    unnamed x26, local copies, waits for them, and re-layouts  9.42 us
  transfers between devices with their start and end apart: 3, of which 3 were waited for; matrix products, arithmetic and copies ran while one was open for 4% of the time, Pallas kernels for 0%

profile of v1, /device:TPU:2, one launch (start us, length us, event | category | flops | bytes accessed | tf_op | source)
XLA Modules:
  0.0 337.1 jit_solution(8648048093821091158)
XLA Ops:
  0.6 0.0 copy-start
  0.6 0.0 copy-start.2
  0.7 1.1 broadcast_in_dim.44
  1.8 19.7 %all_to_all.32 = bf16[4,512,288]{1,2,0:T(8,128)(2,1)S(1)} all-to-all(bf16[4,512,288]{1,2,0:T(8,128)(2,1)S(1)} %broadcast_in_dim.44), channel_id=1, replica_groups=mesh['section'=4,'kv'=16,'tp'=4] {'tp'}, dimensions={0} | all-to-all | bytes 2359296 | tf_op jit(solution)/shard_map/all_to_all | solution.py:26
  21.4 0.0 copy-done.2
  21.4 1.7 stack.2
  23.1 8.6 %all-to-all-start.1 = ((bf16[4,288,1152]{2,1,0:T(8,128)(2,1)}), bf16[4,288,1152]{2,1,0:T(8,128)(2,1)}, u32[]{:S(2)}, u32[]{:S(2)}) async-start(bf16[4,288,1152]{2,1,0:T(8,128)(2,1)} %stack.2), calls=%async_computation.1 | async-start | bytes 5308416 | tf_op jit(solution)/shard_map/all_to_all | solution.py:15
  31.7 0.0 copy-done.3
  31.7 0.1 add.109
  31.8 0.0 copy-done.4
  31.8 0.1 mul.84
  31.9 0.2 convert_reduce_fusion
  32.1 0.4 fusion.10
  32.5 62.6 %all-to-all-done.1 = bf16[4,288,1152]{2,1,0:T(8,128)(2,1)} async-done(((bf16[4,288,1152]{2,1,0:T(8,128)(2,1)}), bf16[4,288,1152]{2,1,0:T(8,128)(2,1)}, u32[]{:S(2)}, u32[]{:S(2)}) %all-to-all-start.1) | async-done | bytes 2654240 | tf_op jit(solution)/shard_map/all_to_all | solution.py:15
  95.1 5.2 %multiply_reduce_fusion = (f32[512]{0:T(512)S(1)}, f32[512,1152]{1,0:T(8,128)}) fusion(f32[1152]{0:T(1024)S(1)} %copy-done.8, bf16[4,288,1152]{2,1,0:T(8,128)(2,1)} %all-to-all-done.1, bf16[4,512,288]{1,2,0:T(8,128)(2,1)S(1)} %all_to_all.32, f32[4,288]{1,0:T(4,128)S(1)} %add.109, f32[4,288]{1,0:T(4,128)S(1)} %mul.84, f32[512]{0:T(512)S(1)} %add_rsqrt_fusion.1, ...), kind=kOutput, calls=%fused_computation.23 | convolution fusion | flops 1364262400 | bytes 6213120 | tf_op jit(solution)/shard_map/dot_general | solution.py:116
  100.4 7.7 %all_to_all.33 = f32[4,1,512]{2,1,0:T(1,128)S(1)} all-to-all(f32[4,1,512]{2,1,0:T(1,128)S(1)} %broadcast_in_dim.45), channel_id=1, replica_groups=mesh['section'=4,'kv'=16,'tp'=4] {'tp'}, dimensions={0} | all-to-all | bytes 16384 | tf_op jit(solution)/shard_map/all_to_all | solution.py:26
  108.1 6.0 %fusion = f32[512,2,1024]{2,0,1:T(8,128)S(1)} fusion(bf16[1152,2,1024]{2,1,0:T(2,128)(2,1)} %param.19, f32[512,1152]{1,0:T(8,128)} %get-tuple-element.11, f32[1152]{0:T(1024)S(1)} %copy-done.9, f32[512]{0:T(512)S(1)} %add_rsqrt_fusion), kind=kOutput, calls=%fused_computation | convolution fusion | flops 2417688576 | bytes 11278848 | tf_op jit(solution)/shard_map/nd,dcf->ncf/dot_general | solution.py:124
  114.2 0.4 copy.162
  114.6 33.0 %all_to_all.34 = f32[4,512,2,256]{3,1,2,0:T(8,128)} all-to-all(f32[4,512,2,256]{3,1,2,0:T(8,128)S(1)} %bitcast.85), channel_id=1, replica_groups=mesh['section'=4,'kv'=16,'tp'=4] {'tp'}, dimensions={0} | all-to-all | bytes 8388608 | tf_op jit(solution)/shard_map/all_to_all | solution.py:45
  147.6 2.5 reduce_sum.99
  150.1 0.4 copy.95
  150.5 0.3 collective-permute-start
  150.8 0.1 reshape.285
  150.9 0.1 copy.89
  151.0 0.1 convert_reduce_fusion.1
  151.1 0.2 add_reduce_fusion
  151.3 12.0 %collective-permute-done = bf16[4,128,2,256]{3,0,2,1:T(4,128)(2,1)S(1)} collective-permute-done((bf16[4,128,2,256]{3,0,2,1:T(4,128)(2,1)S(1)}, bf16[4,128,2,256]{3,0,2,1:T(4,128)(2,1)S(1)}, u32[]{:S(2)}, u32[]{:S(2)}) %collective-permute-start) | collective-permute-done | bytes 524320 | tf_op jit(solution)/shard_map/ppermute | solution.py:52
  163.3 1.4 convolution_convert_fusion
  164.7 6.3 %copy.96 = bf16[32,128,2,256]{3,2,1,0:T(2,128)(2,1)} copy(bf16[32,128,2,256]{3,0,2,1:T(8,128)(2,1)S(1)} %convolution_convert_fusion) | data formatting | bytes 8388608 | tf_op jit(solution)/shard_map/convert_element_type | solution.py:137
  171.0 24.0 %all-to-all-start.4 = ((bf16[32,128,2,256]{3,2,1,0:T(2,128)(2,1)}), bf16[32,128,2,256]{3,2,1,0:T(2,128)(2,1)}, u32[]{:S(2)}, u32[]{:S(2)}) async-start(bf16[32,128,2,256]{3,2,1,0:T(2,128)(2,1)} %copy.96), calls=%async_computation.4 | async-start | bytes 8388608 | tf_op jit(solution)/shard_map/all_to_all | solution.py:136
  195.1 0.1 copy.100
  195.2 0.1 add.117
  195.3 0.1 fusion.50
  195.4 0.2 and_reduce_fusion
  195.6 0.1 broadcast_bitcast_fusion
  195.7 0.0 copy-done.1
  195.7 0.0 copy-start.5
  195.7 10.0 %slice_reduce_fusion.3 = (bf16[16,128,256]{2,1,0:T(8,128)(2,1)}, bf16[16,128,256]{2,1,0:T(8,128)(2,1)S(1)}) fusion(bf16[16,128,2,256]{3,2,1,0:T(2,128)(2,1)S(1)} %copy-done.1), kind=kLoop, calls=%fused_computation.34 | loop fusion | bytes 4194304 | tf_op jit(solution)/shard_map/slice | solution.py:74
  205.7 1.4 reshape.298
  207.1 0.0 copy-done.5
  207.1 0.2 reduce-window_clone.1
  207.3 0.3 reshape.300
  207.6 0.0 copy-done.6
  207.6 0.1 fusion.46
  207.7 0.1 broadcast_bitcast_fusion.1
  207.8 0.5 fusion.53
  208.3 0.3 convolution_bitcast_fusion.1
  208.5 61.4 %all-to-all-done.4 = bf16[32,128,2,256]{3,2,1,0:T(2,128)(2,1)} async-done(((bf16[32,128,2,256]{3,2,1,0:T(2,128)(2,1)}), bf16[32,128,2,256]{3,2,1,0:T(2,128)(2,1)}, u32[]{:S(2)}, u32[]{:S(2)}) %all-to-all-start.4) | async-done | bytes 4194336 | tf_op jit(solution)/shard_map/all_to_all | solution.py:136
  269.9 21.9 %slice_reduce_fusion.1 = (bf16[32,128,256]{2,1,0:T(8,128)(2,1)S(1)}, bf16[32,128,256]{2,1,0:T(8,128)(2,1)}) fusion(bf16[32,128,2,256]{3,2,1,0:T(2,128)(2,1)} %all-to-all-done.4), kind=kLoop, calls=%fused_computation.10 | loop fusion | bytes 8388608 | tf_op jit(solution)/shard_map/slice | solution.py:74
  291.8 2.1 reshape.299
  293.9 2.5 reshape.301
  296.4 2.3 fusion.54
  298.8 0.4 fusion.35
  299.2 0.1 copy.104
  299.3 0.1 add.119
  299.4 0.1 pad_maximum_fusion
  299.5 0.1 broadcast_in_dim.54
  299.6 27.4 %all_to_all.35 = f32[16,1,2064]{2,1,0:T(1,128)S(1)} all-to-all(f32[16,1,2064]{2,1,0:T(1,128)S(1)} %broadcast_in_dim.54), channel_id=1, replica_groups=mesh['section'=4,'kv'=16,'tp'=4] {'kv'}, dimensions={0} | all-to-all | bytes 264192 | tf_op jit(solution)/shard_map/all_to_all | solution.py:26
  326.9 0.1 reduce_sum.103
  327.1 0.1 slice.34
  327.1 0.1 div.69
  327.2 0.1 div.70
  327.3 0.6 divide_convert_fusion
  327.9 9.2 %copy.165 = bf16[32,128,2,256]{3,2,1,0:T(2,128)(2,1)} copy(bf16[32,128,2,256]{3,2,1,0:T(2,128)(2,1)} %all-to-all-done.4) | data formatting | bytes 8388608
  (37 shorter events, 0.3 us)
Async XLA Ops:
  0.6 207.1 %copy-start = (bf16[4,512]{1,0:T(4,128)(2,1)S(1)}, bf16[4,512]{1,0:T(4,128)(2,1)}, u32[]{:S(2)}) copy-start(bf16[4,512]{1,0:T(4,128)(2,1)} %param.20) | copy-start | bytes 12292
  0.6 20.8 %copy-start.2 = (bf16[288,1152]{1,0:T(8,128)(2,1)S(1)}, bf16[288,1152]{1,0:T(8,128)(2,1)}, u32[]{:S(2)}) copy-start(bf16[288,1152]{1,0:T(8,128)(2,1)} %param.16) | copy-start | bytes 1990660
  23.1 8.6 %copy-start.3 = (f32[1152]{0:T(1024)S(1)}, f32[1152]{0:T(1024)}, u32[]{:S(2)}) copy-start(f32[1152]{0:T(1024)} %param.15) | copy-start | bytes 13828
  23.1 8.7 %copy-start.4 = (f32[1152]{0:T(1024)S(1)}, f32[1152]{0:T(1024)}, u32[]{:S(2)}) copy-start(f32[1152]{0:T(1024)} %param.14) | copy-start | bytes 13828
  23.1 72.0 %all-to-all-start.1 = ((bf16[4,288,1152]{2,1,0:T(8,128)(2,1)}), bf16[4,288,1152]{2,1,0:T(8,128)(2,1)}, u32[]{:S(2)}, u32[]{:S(2)}) async-start(bf16[4,288,1152]{2,1,0:T(8,128)(2,1)} %stack.2), calls=%async_computation.1 | async-start | bytes 5308416 | tf_op jit(solution)/shard_map/all_to_all | solution.py:15
  31.7 63.4 %copy-start.8 = (f32[1152]{0:T(1024)S(1)}, f32[1152]{0:T(1024)}, u32[]{:S(2)}) copy-start(f32[1152]{0:T(1024)} %param.17) | copy-start | bytes 13828
  32.5 75.6 %copy-start.9 = (f32[1152]{0:T(1024)S(1)}, f32[1152]{0:T(1024)}, u32[]{:S(2)}) copy-start(f32[1152]{0:T(1024)} %param.18) | copy-start | bytes 13828
  147.6 3.2 copy-start.7
  150.5 12.8 %collective-permute-start = (bf16[4,128,2,256]{3,0,2,1:T(4,128)(2,1)S(1)}, bf16[4,128,2,256]{3,0,2,1:T(4,128)(2,1)S(1)}, u32[]{:S(2)}, u32[]{:S(2)}) collective-permute-start(bf16[4,128,2,256]{3,0,2,1:T(4,128)(2,1)S(1)} %copy.95), channel_id=1, source_target_pairs={{0,64},{64,128},{128,192},{192,0},{1,65},{65,129},{129,193},{193,1... | collective-permute-start | bytes 1572872 | tf_op jit(solution)/shard_map/ppermute | solution.py:52
  171.0 24.3 %copy-start.10 = (s32[1,2]{1,0:T(1,128)S(1)}, s32[1,2]{1,0:T(1,128)}, u32[]{:S(2)}) copy-start(s32[1,2]{1,0:T(1,128)} %param.25) | copy-start | bytes 28
  171.0 24.7 %copy-start.1 = (bf16[16,128,2,256]{3,2,1,0:T(2,128)(2,1)S(1)}, bf16[16,128,2,256]{3,2,1,0:T(2,128)(2,1)}, u32[]{:S(2)}) copy-start(bf16[16,128,2,256]{3,2,1,0:T(2,128)(2,1)} %param.21) | copy-start | bytes 6291460
  171.0 98.8 %all-to-all-start.4 = ((bf16[32,128,2,256]{3,2,1,0:T(2,128)(2,1)}), bf16[32,128,2,256]{3,2,1,0:T(2,128)(2,1)}, u32[]{:S(2)}, u32[]{:S(2)}) async-start(bf16[32,128,2,256]{3,2,1,0:T(2,128)(2,1)} %copy.96), calls=%async_computation.4 | async-start | bytes 8388608 | tf_op jit(solution)/shard_map/all_to_all | solution.py:136
  195.7 11.3 %copy-start.5 = (s32[1,4]{1,0:T(1,128)S(1)}, s32[1,4]{1,0:T(1,128)}, u32[]{:S(2)}) copy-start(s32[1,4]{1,0:T(1,128)} %param.22) | copy-start | bytes 52
  205.7 1.9 copy-start.6
